TPU v7x, 32 devices: a whole 2x2x4 slice. The times are simulated.
32 devices in a mesh: region: 2 (over x), ty: 16 (over z, y, core).
Axes of the slice: x: 2, y: 2, z: 4, core: 2. Of those that a mesh axis runs over, the one named last changes fastest.
Arguments:
- mask_init: float32 [32, 512, 512], P(('region', 'ty')), parts along dimension 0, may hold values from -1.6 to 1.6
- dual_init: float32 [32, 512, 512], P(('region', 'ty')), parts along dimension 0, may hold values from -1.5 to 1.5
- target: bfloat16 [32, 512, 512], P(('region', 'ty')), parts along dimension 0, may hold values from 0 to 1, as said below
- kernels: float32 [8, 2, 1024], replicated, may hold values from -9 to 9
- weights: float32 [8], replicated, may hold values from 0.1 to 1
Outputs:
- mask_final: float32 [32, 512, 512], P(('region', 'ty')), parts along dimension 0
- dual_final: float32 [32, 512, 512], P(('region', 'ty')), parts along dimension 0
There are 2 independent parts, one for each index of `region`. A program takes and returns all parts, laid end to end along the dimension named above; an argument that names none is the same for every part. Nothing has to cross between parts.
Inputs may be any that keep to these rules, and one draw needn't show every extreme that they name: `target`: each entry is 0 or 1; wherever two tiles cover the same canvas position they hold the same value.
All inputs are finite; a program needn't handle non-finite values.
Results may differ from a plain program's by a relative error of at most 0.0045.
Values sent between devices are 32-bit elements; how exact they have to be, the bound alone decides.
A program may use at most 128 MiB of HBM per device.

v0:
```python
import math

import jax
import jax.numpy as jnp
from jax import lax
from jax.sharding import PartitionSpec as P

N = 512
INTERSECTION = 128
F = 32
GRID_COLS = 4
ITERS = 2


SHARPNESS = 8.0
THRESHOLD = 0.3
STEP_SIZE = 0.25
PENALTY = 1.0
PRECISE = lax.Precision.HIGHEST


def passed_along(shard, axis, by):
    count = lax.axis_size(axis)
    pairs = [(i, i + by) for i in range(count) if 0 <= i + by < count]
    return lax.ppermute(shard, axis, pairs)


def tables():
    pixels = jnp.arange(N, dtype=jnp.int32)
    frequencies = jnp.arange(F, dtype=jnp.int32) - F // 2
    phases = frequencies[:, None] * pixels[None, :] % N
    angles = phases.astype(jnp.float32) * (2.0 * math.pi / N)
    return (jnp.cos(angles), -jnp.sin(angles))


def exact_dot(left_side, right_side, contract):
    return lax.dot_general(
        left_side,
        right_side,
        (contract, ((), ())),
        precision=PRECISE,
        preferred_element_type=jnp.float32,
    )


def plain_dot(left_side, right_side, contract):
    return lax.dot_general(
        left_side, right_side, (contract, ((), ())), preferred_element_type=jnp.float32
    )


def kernel_field(kernel, spectrum_real, spectrum_imag, cos_table, sin_table, rows_low):
    kernel_real = kernel[0].reshape(F, F)
    kernel_imag = kernel[1].reshape(F, F)
    gated_real = kernel_real * spectrum_real - kernel_imag * spectrum_imag
    gated_imag = kernel_real * spectrum_imag + kernel_imag * spectrum_real
    band_real = exact_dot(gated_real, cos_table, ((1,), (0,))) + exact_dot(
        gated_imag, sin_table, ((1,), (0,))
    )
    band_imag = exact_dot(gated_imag, cos_table, ((1,), (0,))) - exact_dot(
        gated_real, sin_table, ((1,), (0,))
    )
    upper = jnp.concatenate([band_real, band_imag], axis=1)
    lower = jnp.concatenate([band_imag, -band_real], axis=1)
    stacked = jnp.concatenate([upper, lower], axis=0).astype(jnp.bfloat16)
    return plain_dot(rows_low, stacked, ((0,), (0,))) / (N * N)


def mask_gradient(mask, target, kernels, weights):
    cos_table, sin_table = tables()
    rows_exact = jnp.concatenate([cos_table, sin_table], axis=0)
    rows_low = rows_exact.astype(jnp.bfloat16)
    cos_low = cos_table.astype(jnp.bfloat16)
    sin_low = sin_table.astype(jnp.bfloat16)
    partial_band = plain_dot(rows_low, mask.astype(jnp.bfloat16), ((1,), (1,)))
    part_real = partial_band[:F]
    part_imag = partial_band[F:]
    spectrum_real = exact_dot(cos_table, part_real, ((1,), (1,))) - exact_dot(
        sin_table, part_imag, ((1,), (1,))
    )
    spectrum_imag = exact_dot(cos_table, part_imag, ((1,), (1,))) + exact_dot(
        sin_table, part_real, ((1,), (1,))
    )
    weight_total = jnp.sum(weights)

    def forward(summed, item):
        kernel, weight = item
        field = kernel_field(kernel, spectrum_real, spectrum_imag, cos_table, sin_table, rows_low)
        field_real = field[:, :N]
        field_imag = field[:, N:]
        return (summed + weight * (field_real * field_real + field_imag * field_imag), field)

    summed, fields = lax.scan(forward, jnp.zeros((N, N), jnp.float32), (kernels, weights))
    intensity = summed / weight_total
    resist = jax.nn.sigmoid(SHARPNESS * (intensity - THRESHOLD))
    slope = 2.0 * (resist - target.astype(jnp.float32)) * SHARPNESS * resist * (1.0 - resist)
    slope_wide = jnp.concatenate([slope, slope], axis=1)
    back_table = jnp.concatenate(
        [jnp.concatenate([cos_low, -sin_low], axis=1), jnp.concatenate([sin_low, cos_low], axis=1)],
        axis=0,
    )

    def backward(carry, item):
        adjoint_real, adjoint_imag = carry
        kernel, weight, field = item
        weighted = (slope_wide * field).astype(jnp.bfloat16)
        turned = plain_dot(back_table, weighted, ((1,), (1,)))
        turned_real = turned[:F]
        turned_imag = turned[F:]
        back_real = exact_dot(cos_table, turned_real, ((1,), (1,))) - exact_dot(
            sin_table, turned_imag, ((1,), (1,))
        )
        back_imag = exact_dot(cos_table, turned_imag, ((1,), (1,))) + exact_dot(
            sin_table, turned_real, ((1,), (1,))
        )
        kernel_real = kernel[0].reshape(F, F)
        kernel_imag = kernel[1].reshape(F, F)
        portion = weight / weight_total
        new_real = adjoint_real + portion * (kernel_real * back_real + kernel_imag * back_imag)
        new_imag = adjoint_imag + portion * (kernel_real * back_imag - kernel_imag * back_real)
        return ((new_real, new_imag), None)

    zero_block = jnp.zeros((F, F), jnp.float32)
    adjoints, unused = lax.scan(backward, (zero_block, zero_block), (kernels, weights, fields))
    adjoint_real, adjoint_imag = adjoints
    tail_real = exact_dot(adjoint_real, cos_table, ((1,), (0,))) + exact_dot(
        adjoint_imag, sin_table, ((1,), (0,))
    )
    tail_imag = exact_dot(adjoint_imag, cos_table, ((1,), (0,))) - exact_dot(
        adjoint_real, sin_table, ((1,), (0,))
    )
    tails = jnp.concatenate([tail_real, tail_imag], axis=0)
    return exact_dot(rows_exact, tails, ((0,), (0,))) * (2.0 / (N * N))


def from_peer(piece, offset):
    return passed_along(piece, "ty", offset)


def direct_sum(shared, has_left, has_right, has_upper, has_lower):
    far_edge = N - INTERSECTION
    summed = shared
    summed = summed.at[:, :INTERSECTION].add(has_left * from_peer(shared[:, far_edge:], 1))
    summed = summed.at[:, far_edge:].add(has_right * from_peer(shared[:, :INTERSECTION], -1))
    summed = summed.at[:INTERSECTION, :].add(has_upper * from_peer(shared[far_edge:, :], GRID_COLS))
    summed = summed.at[far_edge:, :].add(
        has_lower * from_peer(shared[:INTERSECTION, :], -GRID_COLS)
    )
    summed = summed.at[:INTERSECTION, :INTERSECTION].add(
        has_upper * has_left * from_peer(shared[far_edge:, far_edge:], GRID_COLS + 1)
    )
    summed = summed.at[:INTERSECTION, far_edge:].add(
        has_upper * has_right * from_peer(shared[far_edge:, :INTERSECTION], GRID_COLS - 1)
    )
    summed = summed.at[far_edge:, :INTERSECTION].add(
        has_lower * has_left * from_peer(shared[:INTERSECTION, far_edge:], 1 - GRID_COLS)
    )
    summed = summed.at[far_edge:, far_edge:].add(
        has_lower * has_right * from_peer(shared[:INTERSECTION, :INTERSECTION], -GRID_COLS - 1)
    )
    return summed


def per_device(mask_init, dual_init, target, kernels, weights):
    mask = mask_init[0]
    dual = dual_init[0]
    goal = target[0]
    device_index = lax.axis_index("ty")
    grid_rows = lax.axis_size("ty") // GRID_COLS
    tile_row = device_index // GRID_COLS
    tile_col = device_index % GRID_COLS
    has_left = (tile_col > 0).astype(jnp.float32)
    has_right = (tile_col < GRID_COLS - 1).astype(jnp.float32)
    has_upper = (tile_row > 0).astype(jnp.float32)
    has_lower = (tile_row < grid_rows - 1).astype(jnp.float32)
    positions = jnp.arange(N, dtype=jnp.int32)
    near_band = (positions < INTERSECTION).astype(jnp.float32)
    far_band = (positions >= N - INTERSECTION).astype(jnp.float32)
    count_rows = 1.0 + has_upper * near_band + has_lower * far_band
    count_cols = 1.0 + has_left * near_band + has_right * far_band
    coverage = count_rows[:, None] * count_cols[None, :]
    for iteration in range(ITERS):
        shared = mask + dual
        summed = direct_sum(shared, has_left, has_right, has_upper, has_lower)
        agreed = summed / coverage
        dual = dual + mask - agreed
        gradient = mask_gradient(mask, goal, kernels, weights)
        mask = mask - STEP_SIZE * (gradient + PENALTY * (mask - agreed + dual))
    return (mask[None], dual[None])


def solution(mesh):
    return jax.shard_map(
        per_device,
        mesh=mesh,
        in_specs=(
            P(("region", "ty"), None, None),
            P(("region", "ty"), None, None),
            P(("region", "ty"), None, None),
            P(),
            P(),
        ),
        out_specs=(P(("region", "ty"), None, None), P(("region", "ty"), None, None)),
        check_vma=False,
    )
```

profile of v0, /device:TPU:1, one launch (start us, length us, event | category | flops | bytes accessed | tf_op | source)
XLA Modules:
  0.0 410.2 jit_solution(15168338503799225687)
XLA Ops:
  3.3 4.6 %collective-permute-start = (f32[512,128]{1,0:T(8,128)}, f32[512,128]{1,0:T(8,128)}, u32[]{:S(2)}, u32[]{:S(2)}) collective-permute-start(f32[512,128]{1,0:T(8,128)} %slice.559), channel_id=1, source_target_pairs={{0,1},{1,2},{2,3},{3,4},{4,5},{5,6},{6,7},{7,8},{8,9},{9,10},{10,1... | collective-permute-start | bytes 786440 | tf_op jit(solution)/shard_map/ppermute | solution.py:25
  8.8 3.9 collective-permute-start.2
  14.7 4.9 %collective-permute-start.4 = (f32[128,128]{1,0:T(8,128)}, f32[128,128]{1,0:T(8,128)}, u32[]{:S(2)}, u32[]{:S(2)}) collective-permute-start(f32[128,128]{1,0:T(8,128)} %get-tuple-element.1069), channel_id=1, source_target_pairs={{0,5},{1,6},{2,7},{3,8},{4,9},{5,10},{6,11},{7,12},{8,13},{9,14},{... | collective-permute-start | bytes 196616 | tf_op jit(solution)/shard_map/ppermute | solution.py:25
  19.6 3.1 collective-permute-start.5
  27.7 7.9 %broadcast.349.clone = f32[8,512,1024]{1,2,0:T(8,128)} broadcast(f32[]{:T(128)} %constant.464.clone.1), dimensions={} | broadcast | bytes 16777220 | tf_op jit(solution)/shard_map/broadcast.27
  35.6 49.3 %while.80 = (s32[]{:T(128)}, f32[512,512]{0,1:T(8,128)S(1)}, f32[8,512,1024]{1,2,0:T(8,128)}, f32[8]{0:T(128)S(1)}, f32[8,2,1024]{2,1,0:T(2,128)S(1)}, /*index=5...) while((s32[]{:T(128)}, f32[512,512]{0,1:T(8,128)S(1)}, ...), condition=%wide.region_1.2_spmd.clone.clone.clone.clone, body=%wide.region_0.1_spmd.clone.clone.clone.clone.sunk | while | flops 96475136 | bytes 13181615 | solution.py:93
  88.8 91.3 %while.81 = (s32[]{:T(128)}, f32[32,32]{0,1:T(8,128)S(1)}, f32[32,32]{0,1:T(8,128)S(1)}, f32[8]{0:T(128)S(1)}, f32[]{:T(128)}, /*index=5*/f32[8,2,1024]{2,1,0:T(...) while((s32[]{:T(128)}, f32[32,32]{0,1:T(8,128)S(1)}, ...), condition=%wide.region_4.5_spmd.clone.clone.clone.clone, body=%wide.region_3.4_spmd.clone.clone.clone.clone.sunk | while | flops 94287872 | bytes 13293763 | solution.py:124
  89.2 3.1 constant_dynamic-slice_fusion.4
  100.6 3.1 constant_dynamic-slice_fusion.4
  112.0 3.1 constant_dynamic-slice_fusion.4
  123.4 3.1 constant_dynamic-slice_fusion.4
  134.8 3.1 constant_dynamic-slice_fusion.4
  146.2 3.1 constant_dynamic-slice_fusion.4
  190.2 4.4 %collective-permute-done.1 = f32[512,128]{1,0:T(8,128)} collective-permute-done((f32[512,128]{1,0:T(8,128)}, f32[512,128]{1,0:T(8,128)}, u32[]{:S(2)}, u32[]{:S(2)}) %collective-permute-start.1) | collective-permute-done | bytes 262176 | tf_op jit(solution)/shard_map/ppermute | solution.py:25
  201.3 3.4 add_select_fusion.7
  204.7 3.5 scatter-add.61
  216.4 7.9 %broadcast.349 = f32[8,512,1024]{1,2,0:T(8,128)} broadcast(f32[]{:T(128)} %constant.464.clone.1), dimensions={} | broadcast | bytes 16777220 | tf_op jit(solution)/shard_map/broadcast.27
  224.3 50.1 %while.82 = (s32[]{:T(128)}, f32[512,512]{0,1:T(8,128)S(1)}, f32[8,512,1024]{1,2,0:T(8,128)}, f32[8]{0:T(128)S(1)}, f32[8,2,1024]{2,1,0:T(2,128)S(1)}, /*index=5...) while((s32[]{:T(128)}, f32[512,512]{0,1:T(8,128)S(1)}, ...), condition=%wide.region_8.9_spmd.clone.clone.clone.clone, body=%wide.region_7.8_spmd.clone.clone.clone.clone.sunk | while | flops 96475136 | bytes 13181615 | solution.py:93
  278.2 91.8 %while.83 = (s32[]{:T(128)}, f32[32,32]{0,1:T(8,128)S(1)}, f32[32,32]{0,1:T(8,128)S(1)}, f32[8]{0:T(128)S(1)}, f32[]{:T(128)}, /*index=5*/f32[8,2,1024]{2,1,0:T(...) while((s32[]{:T(128)}, f32[32,32]{0,1:T(8,128)S(1)}, ...), condition=%wide.region_10.11_spmd.clone.clone.clone.clone, body=%wide.region_9.10_spmd.clone.clone.clone.clone.sunk | while | flops 94287872 | bytes 13293763 | solution.py:124
  290.0 3.1 constant_dynamic-slice_fusion.5
  335.9 3.1 constant_dynamic-slice_fusion.5
  379.5 7.6 %collective-permute-start.10 = (f32[128,512]{1,0:T(8,128)S(1)}, f32[128,512]{1,0:T(8,128)S(1)}, u32[]{:S(2)}, u32[]{:S(2)}) collective-permute-start(f32[128,512]{1,0:T(8,128)S(1)} %get-tuple-element.1063), channel_id=1, source_target_pairs={{0,4},{1,5},{2,6},{3,7},{4,8},{5,9},{6,10},{7,11},{8,12},{9,13},{1... | collective-permute-start | bytes 786440 | tf_op jit(solution)/shard_map/ppermute | solution.py:25
  389.6 4.9 %collective-permute-start.12 = (f32[128,128]{1,0:T(8,128)S(1)}, f32[128,128]{1,0:T(8,128)S(1)}, u32[]{:S(2)}, u32[]{:S(2)}) collective-permute-start(f32[128,128]{1,0:T(8,128)S(1)} %copy-done.21), channel_id=1, source_target_pairs={{0,5},{1,6},{2,7},{3,8},{4,9},{5,10},{6,11},{7,12},{8,13},{9,14},{... | collective-permute-start | bytes 196616 | tf_op jit(solution)/shard_map/ppermute | solution.py:25
  394.5 3.8 collective-permute-start.13
  (551 shorter events, 300.4 us)
Async XLA Ops:
  0.6 23.1 %copy-start.5 = (f32[1,512,512]{2,1,0:T(8,128)S(1)}, f32[1,512,512]{2,1,0:T(8,128)}, u32[]{:S(2)}) copy-start(f32[1,512,512]{2,1,0:T(8,128)} %param.45) | copy-start | bytes 3145732
  3.3 23.7 %copy-start.22 = (f32[8]{0:T(128)S(1)}, f32[8]{0:T(128)}, u32[]{:S(2)}) copy-start(f32[8]{0:T(128)} %param.49) | copy-start | bytes 100
  3.3 180.9 %collective-permute-start = (f32[512,128]{1,0:T(8,128)}, f32[512,128]{1,0:T(8,128)}, u32[]{:S(2)}, u32[]{:S(2)}) collective-permute-start(f32[512,128]{1,0:T(8,128)} %slice.559), channel_id=1, source_target_pairs={{0,1},{1,2},{2,3},{3,4},{4,5},{5,6},{6,7},{7,8},{8,9},{9,10},{10,1... | collective-permute-start | bytes 786440 | tf_op jit(solution)/shard_map/ppermute | solution.py:25
  8.8 188.1 %collective-permute-start.2 = (f32[128,512]{1,0:T(8,128)}, f32[128,512]{1,0:T(8,128)}, u32[]{:S(2)}, u32[]{:S(2)}) collective-permute-start(f32[128,512]{1,0:T(8,128)} %get-tuple-element.1071), channel_id=1, source_target_pairs={{0,4},{1,5},{2,6},{3,7},{4,8},{5,9},{6,10},{7,11},{8,12},{9,13},{1... | collective-permute-start | bytes 786440 | tf_op jit(solution)/shard_map/ppermute | solution.py:25
  12.7 186.7 %collective-permute-start.3 = (f32[128,512]{1,0:T(8,128)}, f32[128,512]{1,0:T(8,128)}, u32[]{:S(2)}, u32[]{:S(2)}) collective-permute-start(f32[128,512]{1,0:T(8,128)} %get-tuple-element.1070), channel_id=1, source_target_pairs={{4,0},{5,1},{6,2},{7,3},{8,4},{9,5},{10,6},{11,7},{12,8},{13,9},{1... | collective-permute-start | bytes 786440 | tf_op jit(solution)/shard_map/ppermute | solution.py:25
  14.7 185.7 %collective-permute-start.4 = (f32[128,128]{1,0:T(8,128)}, f32[128,128]{1,0:T(8,128)}, u32[]{:S(2)}, u32[]{:S(2)}) collective-permute-start(f32[128,128]{1,0:T(8,128)} %get-tuple-element.1069), channel_id=1, source_target_pairs={{0,5},{1,6},{2,7},{3,8},{4,9},{5,10},{6,11},{7,12},{8,13},{9,14},{... | collective-permute-start | bytes 196616 | tf_op jit(solution)/shard_map/ppermute | solution.py:25
  19.6 181.7 %collective-permute-start.5 = (f32[128,128]{1,0:T(8,128)}, f32[128,128]{1,0:T(8,128)}, u32[]{:S(2)}, u32[]{:S(2)}) collective-permute-start(f32[128,128]{1,0:T(8,128)} %get-tuple-element.1068), channel_id=1, source_target_pairs={{0,3},{1,4},{2,5},{3,6},{4,7},{5,8},{6,9},{7,10},{8,11},{9,12},{10... | collective-permute-start | bytes 196616 | tf_op jit(solution)/shard_map/ppermute | solution.py:25
  23.7 186.2 %copy-start.11 = (f32[32,512]{1,0:T(8,128)}, f32[32,512]{1,0:T(8,128)S(1)}, u32[]{:S(2)}) copy-start(f32[32,512]{1,0:T(8,128)S(1)} %get-tuple-element.1078) | copy-start | bytes 196612
  184.1 25.8 %copy-start.1 = (f32[512,512]{1,0:T(8,128)S(1)}, f32[512,512]{1,0:T(8,128)}, u32[]{:S(2)}) copy-start(f32[512,512]{1,0:T(8,128)} %copy-done) | copy-start | bytes 3145732
  184.1 25.8 %copy-start.14 = (f32[32,512]{1,0:T(8,128)S(1)}, f32[32,512]{1,0:T(8,128)}, u32[]{:S(2)}) copy-start(f32[32,512]{1,0:T(8,128)} %copy-done.13) | copy-start | bytes 196612
  186.6 8.0 %collective-permute-start.1 = (f32[512,128]{1,0:T(8,128)}, f32[512,128]{1,0:T(8,128)}, u32[]{:S(2)}, u32[]{:S(2)}) collective-permute-start(f32[512,128]{1,0:T(8,128)} %get-tuple-element.1072), channel_id=1, source_target_pairs={{1,0},{2,1},{3,2},{4,3},{5,4},{6,5},{7,6},{8,7},{9,8},{10,9},{11,1... | collective-permute-start | bytes 786440 | tf_op jit(solution)/shard_map/ppermute | solution.py:25
  194.6 13.6 %collective-permute-start.6 = (f32[128,128]{1,0:T(8,128)}, f32[128,128]{1,0:T(8,128)}, u32[]{:S(2)}, u32[]{:S(2)}) collective-permute-start(f32[128,128]{1,0:T(8,128)} %get-tuple-element.1067), channel_id=1, source_target_pairs={{3,0},{4,1},{5,2},{6,3},{7,4},{8,5},{9,6},{10,7},{11,8},{12,9},{13... | collective-permute-start | bytes 196616 | tf_op jit(solution)/shard_map/ppermute | solution.py:25
  196.9 12.2 %collective-permute-start.7 = (f32[128,128]{1,0:T(8,128)}, f32[128,128]{1,0:T(8,128)}, u32[]{:S(2)}, u32[]{:S(2)}) collective-permute-start(f32[128,128]{1,0:T(8,128)} %get-tuple-element.1066), channel_id=1, source_target_pairs={{5,0},{6,1},{7,2},{8,3},{9,4},{10,5},{11,6},{12,7},{13,8},{14,9},{... | collective-permute-start | bytes 196616 | tf_op jit(solution)/shard_map/ppermute | solution.py:25
  278.2 95.4 %copy-start.4 = (f32[512,512]{1,0:T(8,128)S(1)}, f32[512,512]{1,0:T(8,128)}, u32[]{:S(2)}) copy-start(f32[512,512]{1,0:T(8,128)} %copy-done.3) | copy-start | bytes 3145732
  370.6 5.5 %collective-permute-start.8 = (f32[512,128]{1,0:T(8,128)}, f32[512,128]{1,0:T(8,128)S(1)}, u32[]{:S(2)}, u32[]{:S(2)}) collective-permute-start(f32[512,128]{1,0:T(8,128)} %slice.575), channel_id=1, source_target_pairs={{0,1},{1,2},{2,3},{3,4},{4,5},{5,6},{6,7},{7,8},{8,9},{9,10},{10,1... | collective-permute-start | bytes 786440 | tf_op jit(solution)/shard_map/ppermute | solution.py:25
  373.6 20.8 %copy-start.20 = (f32[128,128]{1,0:T(8,128)S(1)}, f32[128,128]{1,0:T(8,128)}, u32[]{:S(2)}) copy-start(f32[128,128]{1,0:T(8,128)} %get-tuple-element.1060) | copy-start | bytes 196612
  373.8 25.9 %copy-start.19 = (f32[128,128]{1,0:T(8,128)S(1)}, f32[128,128]{1,0:T(8,128)}, u32[]{:S(2)}) copy-start(f32[128,128]{1,0:T(8,128)} %get-tuple-element.1058) | copy-start | bytes 196612
  376.8 21.5 %collective-permute-start.9 = (f32[512,128]{1,0:T(8,128)S(1)}, f32[512,128]{1,0:T(8,128)S(1)}, u32[]{:S(2)}, u32[]{:S(2)}) collective-permute-start(f32[512,128]{1,0:T(8,128)S(1)} %get-tuple-element.1064), channel_id=1, source_target_pairs={{1,0},{2,1},{3,2},{4,3},{5,4},{6,5},{7,6},{8,7},{9,8},{10,9},{11,1... | collective-permute-start | bytes 786440 | tf_op jit(solution)/shard_map/ppermute | solution.py:25
  379.5 20.2 %collective-permute-start.10 = (f32[128,512]{1,0:T(8,128)S(1)}, f32[128,512]{1,0:T(8,128)S(1)}, u32[]{:S(2)}, u32[]{:S(2)}) collective-permute-start(f32[128,512]{1,0:T(8,128)S(1)} %get-tuple-element.1063), channel_id=1, source_target_pairs={{0,4},{1,5},{2,6},{3,7},{4,8},{5,9},{6,10},{7,11},{8,12},{9,13},{1... | collective-permute-start | bytes 786440 | tf_op jit(solution)/shard_map/ppermute | solution.py:25
  388.3 12.8 %collective-permute-start.11 = (f32[128,512]{1,0:T(8,128)S(1)}, f32[128,512]{1,0:T(8,128)S(1)}, u32[]{:S(2)}, u32[]{:S(2)}) collective-permute-start(f32[128,512]{1,0:T(8,128)S(1)} %get-tuple-element.1062), channel_id=1, source_target_pairs={{4,0},{5,1},{6,2},{7,3},{8,4},{9,5},{10,6},{11,7},{12,8},{13,9},{1... | collective-permute-start | bytes 786440 | tf_op jit(solution)/shard_map/ppermute | solution.py:25
  389.6 11.6 %collective-permute-start.12 = (f32[128,128]{1,0:T(8,128)S(1)}, f32[128,128]{1,0:T(8,128)S(1)}, u32[]{:S(2)}, u32[]{:S(2)}) collective-permute-start(f32[128,128]{1,0:T(8,128)S(1)} %copy-done.21), channel_id=1, source_target_pairs={{0,5},{1,6},{2,7},{3,8},{4,9},{5,10},{6,11},{7,12},{8,13},{9,14},{... | collective-permute-start | bytes 196616 | tf_op jit(solution)/shard_map/ppermute | solution.py:25
  394.5 6.8 %collective-permute-start.13 = (f32[128,128]{1,0:T(8,128)S(1)}, f32[128,128]{1,0:T(8,128)S(1)}, u32[]{:S(2)}, u32[]{:S(2)}) collective-permute-start(f32[128,128]{1,0:T(8,128)S(1)} %copy-done.20), channel_id=1, source_target_pairs={{0,3},{1,4},{2,5},{3,6},{4,7},{5,8},{6,9},{7,10},{8,11},{9,12},{10... | collective-permute-start | bytes 196616 | tf_op jit(solution)/shard_map/ppermute | solution.py:25
  398.3 7.4 %collective-permute-start.14 = (f32[128,128]{1,0:T(8,128)}, f32[128,128]{1,0:T(8,128)S(1)}, u32[]{:S(2)}, u32[]{:S(2)}) collective-permute-start(f32[128,128]{1,0:T(8,128)} %get-tuple-element.1059), channel_id=1, source_target_pairs={{3,0},{4,1},{5,2},{6,3},{7,4},{8,5},{9,6},{10,7},{11,8},{12,9},{13... | collective-permute-start | bytes 196616 | tf_op jit(solution)/shard_map/ppermute | solution.py:25
  399.7 7.0 %collective-permute-start.15 = (f32[128,128]{1,0:T(8,128)S(1)}, f32[128,128]{1,0:T(8,128)S(1)}, u32[]{:S(2)}, u32[]{:S(2)}) collective-permute-start(f32[128,128]{1,0:T(8,128)S(1)} %copy-done.19), channel_id=1, source_target_pairs={{5,0},{6,1},{7,2},{8,3},{9,4},{10,5},{11,6},{12,7},{13,8},{14,9},{... | collective-permute-start | bytes 196616 | tf_op jit(solution)/shard_map/ppermute | solution.py:25
  (25 other events, 120.3 us)
where the time goes:
time: 415 us; the launch traced here: 410 us
  matrix products  143 us (34%)
  local copies, waits for them, and re-layouts  137 us (33%)
  other arithmetic  50.8 us (12%)
  starting transfers between devices  47.1 us (11%)
  loops' own time  23.5 us (6%)
  waiting for transfers between devices  7.74 us (2%)
    dot_general x146, matrix products, exact_dot(): lax.dot_general(left_side, right_side, (contract, ((), ())), precision=PR...  80.5 us
    dynamic_slice x32, local copies, waits for them, and re-layouts, mask_gradient(): lax.scan(backward, (zero_block, zero_block), (kernels, weights, fields))  80.4 us
    dot_general x34, matrix products, plain_dot(): lax.dot_general(left_side, right_side, (contract, ((), ())), preferred_el...  62.3 us
    ppermute x16, starting transfers between devices, passed_along(): return lax.ppermute(shard, axis, pairs)  47.1 us
    another operation x2, loops' own time, mask_gradient(): lax.scan(backward, (zero_block, zero_block), (kernels, weights, fields))  22.5 us
    dynamic_slice x32, local copies, waits for them, and re-layouts, mask_gradient(): lax.scan(forward, jnp.zeros((N, N), jnp.float32), (kernels, weights))  20.1 us
    add x16, other arithmetic, forward(): summed + weight * (field_real * field_real + field_imag * field_imag)  20 us
    another operation x3, local copies, waits for them, and re-layouts  16.5 us
  transfers between devices with their start and end apart: 16, of which 3 were waited for; matrix products, arithmetic and copies ran while one was open for 42% of the time, Pallas kernels for 0%

commit v1 on v0

v1 whole, which is shorter than its diff:
```python
import functools

import jax
import jax.numpy as jnp
import numpy as np
from jax import lax
from jax.experimental import pallas as pl
from jax.experimental.pallas import tpu as pltpu
from jax.sharding import PartitionSpec as P

GRID_COLS = 4
INTERSECTION = 128
SHARPNESS = 8.0
THRESHOLD = 0.3
STEP_SIZE = 0.25
PENALTY = 1.0
MESH = pl.DeviceIdType.MESH
BF16 = jnp.bfloat16


def split_host(table):
    table = table.astype(np.float32)
    high = table.astype(BF16)
    low = (table - high.astype(np.float32)).astype(BF16)
    return high, low


def host_tables(n, f):
    g = 2 * f
    freq = np.arange(f) - f // 2
    phase = 2.0 * np.pi * ((freq[:, None] * np.arange(n)[None, :]) % n) / n
    cos, sin = np.cos(phase), -np.sin(phase)
    rows = np.concatenate([cos, sin], 0)
    rows_hi, rows_lo = split_host(rows)
    row_side = np.concatenate([rows_hi, rows_lo], 0)
    col_wide = np.concatenate([np.tile(cos.T, (1, 4)), np.tile(sin.T, (1, 4))], 1)
    col_side = split_host(col_wide)[0]
    coarse = 2.0 * np.pi * ((np.arange(g)[:, None] * freq[None, :]) % g) / g
    er, ei = np.cos(coarse), np.sin(coarse)
    pair = np.eye(2)
    to_real = np.kron(pair, np.concatenate([er.T, -ei.T], 0))
    to_imag = np.kron(pair, np.concatenate([ei.T, er.T], 0))
    lane_turn = np.concatenate([to_real, to_imag], 1)
    lane_fwd = np.concatenate(split_host(lane_turn / (n * n)), 1)
    lane_back = np.concatenate(split_host(lane_turn.T), 1)
    row_turn = np.concatenate([np.concatenate([er, -ei], 1), np.concatenate([ei, er], 1)], 0)
    turn_hi, turn_lo = split_host(row_turn)
    row_fwd = np.concatenate([turn_hi, turn_lo, turn_hi, turn_lo], 1)
    row_back = np.concatenate(split_host(row_turn.T), 0)
    half = np.arange(-(f - 1), f)
    angle = np.arange(n)[:, None] * f * 2 - np.arange(g)[None, :] * n
    spread = np.cos(2.0 * np.pi * ((angle[..., None] * half) % (n * g)) / (n * g)).sum(-1) / g
    s_hi, s_lo = split_host(spread)
    up_cols = np.concatenate([s_hi.T, s_lo.T, s_hi.T, s_lo.T], 0)
    er_low, ei_low = rows_hi[:f].T, -rows_hi[f:].T
    low_turn = np.concatenate([np.concatenate([er_low, -ei_low], 1), np.concatenate([ei_low, er_low], 1)], 0)
    up_rows = np.concatenate([low_turn, low_turn], 1)
    down_cols = np.concatenate([s_hi, s_hi, s_lo, s_lo], 1)
    scale = 2.0 / (n * n)
    c_hi, c_lo = split_host(cos * scale)
    t_hi, t_lo = split_host(sin * scale)
    tail_r = np.concatenate([c_hi, c_lo, t_hi, t_lo], 0)
    tail_i = np.concatenate([-t_hi, -t_lo, c_hi, c_lo], 0)
    tail = np.concatenate([tail_r, tail_i], 1)
    tail_tab = np.concatenate([tail, tail], 0)
    grad_rows = np.concatenate([rows_hi.T, rows_lo.T, rows_hi.T, rows_lo.T], 1)
    return [
        np.asarray(t, dtype=BF16)
        for t in (row_side, col_side, lane_fwd, row_fwd, up_cols, up_rows, down_cols, row_back, lane_back, tail_tab, grad_rows)
    ]


def dot(a, b):
    return lax.dot_general(a, b, (((1,), (0,)), ((), ())), preferred_element_type=jnp.float32)


def split(x):
    high = x.astype(BF16)
    return high, (x - high.astype(jnp.float32)).astype(BF16)


def stacked(x):
    high, low = split(x)
    return jnp.concatenate([high, high, low, low], axis=0)


def body(
    n, f, edge, count,
    mask_ref, dual_ref, target_ref, h_ref, w_ref,
    row_side, col_side, lane_fwd, row_fwd, up_cols, up_rows, down_cols, row_back, lane_back, tail_tab, grad_rows,
    mask_out, dual_out,
    shared, ring_s, ring_m, from_h_s, from_h_m, from_v_s, from_v_m, agreed, slope, adj, adj_in,
    send_sem, recv_sem,
):
    far = n - edge
    g = 2 * f
    me = lax.axis_index("ty")
    row, col = me // GRID_COLS, me % GRID_COLS
    grid_rows = count // GRID_COLS
    left, right = col > 0, col < GRID_COLS - 1
    upper, lower = row > 0, row < grid_rows - 1
    near = [
        (-1, left), (1, right), (-GRID_COLS, upper), (GRID_COLS, lower),
        (-GRID_COLS - 1, jnp.logical_and(upper, left)), (-GRID_COLS + 1, jnp.logical_and(upper, right)),
        (GRID_COLS - 1, jnp.logical_and(lower, left)), (GRID_COLS + 1, jnp.logical_and(lower, right)),
    ]
    opposite = [1, 0, 3, 2, 7, 6, 5, 4]

    barrier = pltpu.get_barrier_semaphore()
    for shift, there in near:
        @pl.when(there)
        def _(shift=shift):
            pl.semaphore_signal(barrier, inc=1, device_id={"ty": me + shift}, device_id_type=MESH)

    counter = [0]

    def remote(src, dst, to):
        index = counter[0]
        counter[0] += 1
        copy = pltpu.make_async_remote_copy(
            src_ref=src, dst_ref=dst, send_sem=send_sem.at[index], recv_sem=recv_sem.at[index],
            device_id={"ty": me + near[to][0]}, device_id_type=MESH,
        )
        return copy, near[to][1], near[opposite[to]][1]

    def start(entry):
        pl.when(entry[1])(entry[0].start)

    def arrived(entry):
        pl.when(entry[2])(entry[0].wait_recv)

    def sent(entry):
        pl.when(entry[1])(entry[0].wait_send)

    bands = (pl.ds(0, edge), pl.ds(far, edge))
    middle = pl.ds(edge, far - edge)

    def side_copies(src, dst, rows):
        return [
            remote(src.at[rows, bands[0]], dst.at[1, rows, :], 0),
            remote(src.at[rows, bands[1]], dst.at[0, rows, :], 1),
        ]

    src_mask = mask_ref.at[0]
    plan = {}
    for name, src, from_h, from_v, ring in (
        ("s", shared, from_h_s, from_v_s, ring_s),
        ("m", src_mask, from_h_m, from_v_m, ring_m),
    ):
        plan[name, "h"] = side_copies(src, from_h, bands[0]) + side_copies(src, from_h, bands[1])
        plan[name, "hm"] = side_copies(src, from_h, middle)
        plan[name, "v"] = [
            remote(src.at[bands[0], middle], from_v.at[1, :, middle], 2),
            remote(src.at[bands[1], middle], from_v.at[0, :, middle], 3),
        ]
        plan[name, "vc"] = [
            remote(ring.at[v, h], from_v.at[1 - v, :, bands[h]], 2 + v) for v in range(2) for h in range(2)
        ]
    plan["adj"] = [remote(adj, adj_in.at[opposite[to]], to) for to in range(8)]

    for h in range(2):
        @pl.when(jnp.logical_not(near[h][1]))
        def _(h=h):
            from_h_s[h] = jnp.zeros((n, edge), jnp.float32)
            from_h_m[h] = jnp.zeros((n, edge), jnp.float32)

        @pl.when(jnp.logical_not(near[2 + h][1]))
        def _(h=h):
            from_v_s[h] = jnp.zeros((edge, n), jnp.float32)
            from_v_m[h] = jnp.zeros((edge, n), jnp.float32)
    for to in range(8):
        @pl.when(jnp.logical_not(near[to][1]))
        def _(to=to):
            adj_in[to] = jnp.zeros((f, 4 * f), jnp.float32)

    shared[...] = mask_ref[0] + dual_ref[0]
    expected = sum(there.astype(jnp.int32) for _, there in near)
    pl.semaphore_wait(barrier, expected)

    for entry in plan["s", "h"] + plan["s", "v"] + plan["s", "hm"]:
        start(entry)

    quarters = w_ref.shape[0] // 2
    lane = lax.broadcasted_iota(jnp.int32, (1, 4 * f), 1)
    total = w_ref[0]
    for k in range(1, w_ref.shape[0]):
        total = total + w_ref[k]
    portions = [
        jnp.where(lane < 2 * f, w_ref[2 * k], w_ref[2 * k + 1]) / jnp.full((1, 4 * f), total, jnp.float32)
        for k in range(quarters)
    ]
    h_one = h_ref[...]
    is_real = (lane // f) % 2 == 0
    h_two = jnp.where(is_real, -pltpu.roll(h_one, 3 * f, 1), pltpu.roll(h_one, f, 1))

    def fields(mask_low):
        part = dot(row_side[...], mask_low)
        part = part[: 2 * f] + part[2 * f :]
        grid = dot(jnp.concatenate(split(part), axis=0), col_side[...])
        w = 8 * f
        grid = grid[: 2 * f] + grid[2 * f :]
        real = grid[:f, : 4 * f] - grid[f:, 4 * f :]
        imag = grid[:f, 4 * f :] + grid[f:, : 4 * f]
        real = jnp.concatenate([real] * quarters, axis=0)
        imag = jnp.concatenate([imag] * quarters, axis=0)
        gated = h_one * real + h_two * imag
        turned = dot(jnp.concatenate(split(gated), axis=0), lane_fwd[...])
        m = quarters * f
        turned = (turned[:m, :w] + turned[:m, w:]) + turned[m:, :w]
        wide = jnp.concatenate(
            [
                jnp.concatenate([turned[k * f : (k + 1) * f, : 4 * f], turned[k * f : (k + 1) * f, 4 * f :]], axis=0)
                for k in range(quarters)
            ],
            axis=1,
        )
        return dot(row_fwd[...], stacked(wide)), jnp.concatenate(split(wide), axis=0)

    def write_slope(waves):
        for r in range(0, n, edge):
            real = dot(up_rows[r : r + edge, :], waves)
            imag = dot(up_rows[n + r : n + r + edge, :], waves)
            energy = real * real + imag * imag
            summed = energy[:, : 2 * g] * portions[0]
            for k in range(1, quarters):
                summed = summed + energy[:, 2 * g * k : 2 * g * (k + 1)] * portions[k]
            summed = summed + pltpu.roll(summed, g, 1)
            intensity = dot(jnp.concatenate(split(summed), axis=1), up_cols[...])
            resist = 1.0 / (1.0 + jnp.exp(-SHARPNESS * (intensity - THRESHOLD)))
            goal = target_ref[0, r : r + edge, :].astype(jnp.float32)
            value = (2.0 * SHARPNESS) * (resist - goal) * resist * (1.0 - resist)
            slope[r : r + edge, :] = value.astype(BF16)

    def adjoint(field):
        low = dot(up_cols[: 2 * g, :], slope[...])
        low = low[:g] + low[g:]
        low = dot(jnp.concatenate(split(low), axis=0), down_cols[...])
        low = (low[:g, : 2 * g] + low[:g, 2 * g :]) + low[g:, : 2 * g]
        weighted = field * jnp.concatenate([jnp.concatenate([low] * quarters, axis=1)] * 2, axis=0)
        high, rest = split(weighted)
        back = dot(row_back[...], high)
        back = (back[: 2 * f] + back[2 * f :]) + dot(row_back[: 2 * f, :], rest)
        tall = jnp.concatenate(
            [
                jnp.concatenate([back[:f, 4 * f * k : 4 * f * (k + 1)], back[f:, 4 * f * k : 4 * f * (k + 1)]], axis=1)
                for k in range(quarters)
            ],
            axis=0,
        )
        m = quarters * f
        turned = dot(jnp.concatenate(split(tall), axis=0), lane_back[...])
        turned = (turned[:m, : 4 * f] + turned[:m, 4 * f :]) + turned[m:, : 4 * f]
        first, second = h_one * turned, h_two * turned
        real = jnp.zeros((f, 4 * f), jnp.float32)
        imag = jnp.zeros((f, 4 * f), jnp.float32)
        for k in range(quarters):
            real = real + first[k * f : (k + 1) * f] * portions[k]
            imag = imag + second[k * f : (k + 1) * f] * portions[k]
        real = real + pltpu.roll(real, 2 * f, 1)
        real = real + pltpu.roll(real, f, 1)
        imag = imag + pltpu.roll(imag, 2 * f, 1)
        imag = imag + pltpu.roll(imag, f, 1)
        return jnp.where(lane < 2 * f, real, imag)

    def tails(packed):
        out = dot(jnp.concatenate(split(packed), axis=1), tail_tab[...])
        return out[:, :n], out[:, n:]

    def corners(name, src, from_h, ring):
        for entry in plan[name, "h"]:
            arrived(entry)
        for v in range(2):
            for h in range(2):
                ring[v, h] = src[bands[v], bands[h]] + from_h[h, bands[v], :]
        for entry in plan[name, "vc"]:
            start(entry)

    up_f, down_f = upper.astype(jnp.float32), lower.astype(jnp.float32)
    left_f, right_f = left.astype(jnp.float32), right.astype(jnp.float32)

    def coverage_part(r):
        at_col = lax.broadcasted_iota(jnp.int32, (1, n), 1)
        cols = jnp.where(at_col < edge, 1.0 - 0.5 * left_f, jnp.where(at_col >= far, 1.0 - 0.5 * right_f, 1.0))
        if r == 0:
            return cols * (1.0 - 0.5 * up_f)
        if r == far:
            return cols * (1.0 - 0.5 * down_f)
        return cols

    def covered(src, from_h, from_v, r):
        rows = slice(r, r + edge)
        own = src[rows, :]
        own = jnp.concatenate(
            [own[:, :edge] + from_h[0, rows, :], own[:, edge:far], own[:, far:] + from_h[1, rows, :]], axis=1
        )
        if r == 0:
            own = own + from_v[0]
        if r == far:
            own = own + from_v[1]
        return own * coverage_part(r)

    field, waves = fields(mask_ref[0].astype(BF16))
    write_slope(waves)
    corners("s", shared, from_h_s, ring_s)
    for entry in plan["m", "h"] + plan["m", "v"] + plan["m", "hm"]:
        start(entry)
    packed = adjoint(field)
    adj[...] = packed
    tail_own = tails(packed)
    own_stack = stacked(jnp.concatenate(tail_own, axis=0))
    for entry in plan["s", "hm"] + plan["s", "v"] + plan["s", "vc"]:
        arrived(entry)
    for entry in plan["adj"]:
        start(entry)
    for r in range(0, n, edge):
        rows = slice(r, r + edge)
        gradient = dot(grad_rows[rows, :], own_stack)
        share = shared[rows, :]
        common = covered(shared, from_h_s, from_v_s, r)
        agreed[rows, :] = common
        dual = share - common
        dual_out[0, rows, :] = dual
        mask = mask_ref[0, rows, :]
        mask_out[0, rows, :] = mask - STEP_SIZE * (gradient + PENALTY * (mask - common + dual))

    field, waves = fields(mask_out[0].astype(BF16))
    corners("m", src_mask, from_h_m, ring_m)
    write_slope(waves)
    packed = adjoint(field)
    last_stack = stacked(jnp.concatenate(tails(packed), axis=0))

    for entry in plan["adj"]:
        arrived(entry)

    def joined(tail, tail_left, tail_right):
        return jnp.concatenate(
            [
                jnp.concatenate(
                    [a[:, :edge] + b[:, far:], a[:, edge:far], a[:, far:] + c[:, :edge]], axis=1
                )
                for a, b, c in zip(tail, tail_left, tail_right)
            ],
            axis=0,
        )

    around = [tails(adj_in[to]) for to in range(8)]
    sum_own = stacked(joined(tail_own, around[0], around[1]))
    sum_up = stacked(joined(around[2], around[4], around[5]))
    sum_down = stacked(joined(around[3], around[6], around[7]))
    for entry in plan["m", "hm"] + plan["m", "v"] + plan["m", "vc"]:
        arrived(entry)
    for r in range(0, n, edge):
        rows = slice(r, r + edge)
        summed = dot(grad_rows[rows, :], sum_own)
        if r == 0:
            summed = summed + dot(grad_rows[far:, :], sum_up)
        if r == far:
            summed = summed + dot(grad_rows[:edge, :], sum_down)
        before = agreed[rows, :]
        mean_mask = covered(src_mask, from_h_m, from_v_m, r)
        common = mean_mask - STEP_SIZE * (summed * coverage_part(r) + PENALTY * (mean_mask - before))
        mask = mask_out[0, rows, :]
        dual = dual_out[0, rows, :] + mask - common
        dual_out[0, rows, :] = dual
        gradient = dot(grad_rows[rows, :], last_stack)
        mask_out[0, rows, :] = mask - STEP_SIZE * (gradient + PENALTY * (mask - common + dual))

    for name in ("s", "m"):
        for part in ("h", "hm", "v", "vc"):
            for entry in plan[name, part]:
                sent(entry)
    for entry in plan["adj"]:
        sent(entry)


def per_device(count, mask_init, dual_init, target, kernels, weights):
    n = mask_init.shape[-1]
    edge = INTERSECTION
    f = int(round(kernels.shape[-1] ** 0.5))
    quarters = kernels.shape[0] // 2
    tables = [jnp.asarray(t) for t in host_tables(n, f)]
    arranged = kernels.reshape(quarters, 2, 2, f, f).transpose(0, 3, 1, 2, 4).reshape(quarters * f, 4 * f)
    f32 = jnp.float32
    whole = pl.BlockSpec(memory_space=pltpu.VMEM)
    return pl.pallas_call(
        functools.partial(body, n, f, edge, count),
        out_shape=(jax.ShapeDtypeStruct((1, n, n), f32), jax.ShapeDtypeStruct((1, n, n), f32)),
        in_specs=[whole] * 4 + [pl.BlockSpec(memory_space=pltpu.SMEM)] + [whole] * len(tables),
        out_specs=(whole, whole),
        scratch_shapes=[
            pltpu.VMEM((n, n), f32),
            pltpu.VMEM((2, 2, edge, edge), f32),
            pltpu.VMEM((2, 2, edge, edge), f32),
            pltpu.VMEM((2, n, edge), f32),
            pltpu.VMEM((2, n, edge), f32),
            pltpu.VMEM((2, edge, n), f32),
            pltpu.VMEM((2, edge, n), f32),
            pltpu.VMEM((n, n), f32),
            pltpu.VMEM((n, n), BF16),
            pltpu.VMEM((f, 4 * f), f32),
            pltpu.VMEM((8, f, 4 * f), f32),
            pltpu.SemaphoreType.DMA((40,)),
            pltpu.SemaphoreType.DMA((40,)),
        ],
        compiler_params=pltpu.CompilerParams(
            collective_id=0, has_side_effects=True, vmem_limit_bytes=48 * 1024 * 1024
        ),
    )(mask_init, dual_init, target, arranged, weights, *tables)


def solution(mesh):
    tile = P(("region", "ty"), None, None)
    return jax.shard_map(
        functools.partial(per_device, mesh.shape["ty"]),
        mesh=mesh,
        in_specs=(tile, tile, tile, P(), P()),
        out_specs=(tile, tile),
        check_vma=False,
    )
```

time: 415 us -> 36.2 us (0.09); the launches traced: 410 us -> 35.6 us
  matrix products: 143 us -> 0 us
  local copies, waits for them, and re-layouts: 137 us -> 14.4 us
  other arithmetic: 50.8 us -> 0 us
  starting transfers between devices: 47.1 us -> 0 us
  loops' own time: 23.5 us -> 0 us
  Pallas kernels: 0 us -> 20.5 us
  waiting for transfers between devices: 7.74 us -> 0 us
    dot_general x180 -> x0, matrix products: 143 us -> none  [the longest x146 80.5 us: exact_dot(): lax.dot_general(left_side, right_side, (contract, ((), ())), precision=PR...]
    dynamic_slice x64 -> x0, local copies, waits for them, and re-layouts: 101 us -> none  [the longest x32 80.4 us: mask_gradient(): lax.scan(backward, (zero_block, zero_block), (kernels, weights, fields))]
    ppermute x16 -> x0, starting transfers between devices: 47.1 us -> none  [passed_along(): return lax.ppermute(shard, axis, pairs)]
    another operation x4 -> x0, loops' own time: 23.5 us -> none  [the longest x2 22.5 us: mask_gradient(): lax.scan(backward, (zero_block, zero_block), (kernels, weights, fields))]
    add x35 -> x0, other arithmetic: 22.1 us -> none  [the longest x16 20 us: forward(): summed + weight * (field_real * field_real + field_imag * field_imag)]
    pallas_call x0 -> x1, Pallas kernels: none -> 20.5 us  [per_device(): pl.pallas_call(functools.partial(body, n, f, edge, count), out_shape=(jax...]
    another operation x3 -> x0, local copies, waits for them, and re-layouts: 16.5 us -> none
    unnamed x67 -> x30, local copies, waits for them, and re-layouts: 1.6 us -> 12.8 us
  transfers between devices with their start and end apart: 16 -> 0, of which waited for: 3 -> 0; matrix products, arithmetic and copies ran while one was open for 42% -> 0% of each run, Pallas kernels for 0% -> 0%
where the time goes in v1:
time: 36.2 us; the launch traced here: 35.6 us
  Pallas kernels  20.5 us (57%)
  local copies, waits for them, and re-layouts  14.4 us (40%)
  between operations  0.69 us (2%)
    pallas_call x1, Pallas kernels, per_device(): pl.pallas_call(functools.partial(body, n, f, edge, count), out_shape=(jax...  20.5 us
    unnamed x30, local copies, waits for them, and re-layouts  12.8 us
    reshape x3, local copies, waits for them, and re-layouts, per_device(): kernels.reshape(quarters, 2, 2, f, f).transpose(0, 3, 1, 2, 4)  1.52 us

profile of v1, /device:TPU:1, one launch (start us, length us, event | category | flops | bytes accessed | tf_op | source)
XLA Modules:
  0.0 35.6 jit_solution(2632454088873435269)
XLA Ops:
  0.6 0.0 copy-start
  0.6 1.1 %reshape.10 = f32[4,2,2,32,32]{4,3,2,1,0:T(8,128)S(1)} reshape(f32[8,2,1024]{2,1,0:T(2,128)} %param.19) | data formatting | bytes 131072 | tf_op jit(solution)/shard_map/reshape | solution.py:382
  1.7 0.2 copy.20
  1.9 0.0 copy-start.8
  2.0 0.0 copy-start.13
  2.0 0.2 reshape.11.h_ref
  2.2 0.0 copy-done
  2.2 0.6 %copy-done.8 = bf16[256,256]{1,0:T(8,128)(2,1)S(1)} copy-done((bf16[256,256]{1,0:T(8,128)(2,1)S(1)}, bf16[256,256]{1,0:T(8,128)(2,1)}, u32[]{:S(2)}) %copy-start.8) | copy-done | bytes 131096
  2.8 0.0 copy-done.13
  2.8 0.0 copy-start.1
  2.9 1.0 %copy-done.1 = bf16[1,512,512]{2,1,0:T(8,128)(2,1)S(1)} copy-done((bf16[1,512,512]{2,1,0:T(8,128)(2,1)S(1)}, bf16[1,512,512]{2,1,0:T(8,128)(2,1)}, u32[]{:S(2)}) %copy-start.1) | copy-done | bytes 524312
  3.9 1.0 %copy-done.2 = bf16[256,1024]{1,0:T(8,128)(2,1)S(1)} copy-done((bf16[256,1024]{1,0:T(8,128)(2,1)S(1)}, bf16[256,1024]{1,0:T(8,128)(2,1)}, u32[]{:S(2)}) %copy-start.2) | copy-done | bytes 524312
  4.9 0.9 %copy-done.3 = bf16[512,256]{1,0:T(8,128)(2,1)S(1)} copy-done((bf16[512,256]{1,0:T(8,128)(2,1)S(1)}, bf16[512,256]{1,0:T(8,128)(2,1)}, u32[]{:S(2)}) %copy-start.3) | copy-done | bytes 262168
  5.9 0.9 %copy-done.4 = bf16[512,256]{1,0:T(8,128)(2,1)S(1)} copy-done((bf16[512,256]{1,0:T(8,128)(2,1)S(1)}, bf16[512,256]{1,0:T(8,128)(2,1)}, u32[]{:S(2)}) %copy-start.4) | copy-done | bytes 262168
  6.8 0.9 %copy-done.5 = bf16[1024,128]{1,0:T(8,128)(2,1)S(1)} copy-done((bf16[1024,128]{1,0:T(8,128)(2,1)S(1)}, bf16[1024,128]{1,0:T(8,128)(2,1)}, u32[]{:S(2)}) %copy-start.5) | copy-done | bytes 262168
  7.8 0.9 %copy-done.6 = bf16[256,512]{1,0:T(8,128)(2,1)S(1)} copy-done((bf16[256,512]{1,0:T(8,128)(2,1)S(1)}, bf16[256,512]{1,0:T(8,128)(2,1)}, u32[]{:S(2)}) %copy-start.6) | copy-done | bytes 262168
  8.7 0.9 %copy-done.7 = bf16[512,256]{1,0:T(8,128)(2,1)S(1)} copy-done((bf16[512,256]{1,0:T(8,128)(2,1)S(1)}, bf16[512,256]{1,0:T(8,128)(2,1)}, u32[]{:S(2)}) %copy-start.7) | copy-done | bytes 262168
  9.7 0.9 %copy-done.9 = bf16[128,512]{1,0:T(8,128)(2,1)S(1)} copy-done((bf16[128,512]{1,0:T(8,128)(2,1)S(1)}, bf16[128,512]{1,0:T(8,128)(2,1)}, u32[]{:S(2)}) %copy-start.9) | copy-done | bytes 131096
  10.6 0.9 %copy-done.10 = bf16[128,512]{1,0:T(8,128)(2,1)S(1)} copy-done((bf16[128,512]{1,0:T(8,128)(2,1)S(1)}, bf16[128,512]{1,0:T(8,128)(2,1)}, u32[]{:S(2)}) %copy-start.10) | copy-done | bytes 131096
  11.5 0.8 %copy-done.11 = bf16[128,256]{1,0:T(8,128)(2,1)S(1)} copy-done((bf16[128,256]{1,0:T(8,128)(2,1)S(1)}, bf16[128,256]{1,0:T(8,128)(2,1)}, u32[]{:S(2)}) %copy-start.11) | copy-done | bytes 65560
  12.3 0.8 %copy-done.12 = bf16[128,128]{1,0:T(8,128)(2,1)S(1)} copy-done((bf16[128,128]{1,0:T(8,128)(2,1)S(1)}, bf16[128,128]{1,0:T(8,128)(2,1)}, u32[]{:S(2)}) %copy-start.12) | copy-done | bytes 32792
  13.1 20.5 %shard_map.167 = (f32[1,512,512]{2,1,0:T(8,128)S(1)}, f32[1,512,512]{2,1,0:T(8,128)S(1)}) custom-call(f32[1,512,512]{2,1,0:T(8,128)S(1)} %copy-done, f32[1,512,512]{2,1,0:T(8,128)} %dual_ref.1, bf16[1,512,512]{2,1,0:T(8,128)(2,1)S(1)} %copy-done.1, f32[128,128]{1,0:T(8,128)S(1)} %reshape.11.h_ref, f32[8]{0:T(128)S(1)} %copy-done.13, ...), custom_call_target="tpu_custom_call" | custom-call | tf_op jit(solution)/shard_map/pallas_call | solution.py:385
  33.6 1.0 %copy.23 = f32[1,512,512]{2,1,0:T(8,128)} copy(f32[1,512,512]{2,1,0:T(8,128)S(1)} %get-tuple-element.4) | data formatting | bytes 2097152
  34.6 1.0 %copy.24 = f32[1,512,512]{2,1,0:T(8,128)} copy(f32[1,512,512]{2,1,0:T(8,128)S(1)} %get-tuple-element.5) | data formatting | bytes 2097152
  (10 shorter events, 0.0 us)
Async XLA Ops:
  0.6 1.6 %copy-start = (f32[1,512,512]{2,1,0:T(8,128)S(1)}, f32[1,512,512]{2,1,0:T(8,128)}, u32[]{:S(2)}) copy-start(f32[1,512,512]{2,1,0:T(8,128)} %mask_ref.1) | copy-start | bytes 3145732
  1.9 0.9 %copy-start.8 = (bf16[256,256]{1,0:T(8,128)(2,1)S(1)}, bf16[256,256]{1,0:T(8,128)(2,1)}, u32[]{:S(2)}) copy-start(bf16[256,256]{1,0:T(8,128)(2,1)} %constant.30.clone.lane_back) | copy-start | bytes 393220
  2.0 0.9 %copy-start.13 = (f32[8]{0:T(128)S(1)}, f32[8]{0:T(128)}, u32[]{:S(2)}) copy-start(f32[8]{0:T(128)} %w_ref.1) | copy-start | bytes 100
  2.8 1.0 %copy-start.1 = (bf16[1,512,512]{2,1,0:T(8,128)(2,1)S(1)}, bf16[1,512,512]{2,1,0:T(8,128)(2,1)}, u32[]{:S(2)}) copy-start(bf16[1,512,512]{2,1,0:T(8,128)(2,1)} %target_ref.1) | copy-start | bytes 1572868
  3.9 1.0 %copy-start.2 = (bf16[256,1024]{1,0:T(8,128)(2,1)S(1)}, bf16[256,1024]{1,0:T(8,128)(2,1)}, u32[]{:S(2)}) copy-start(bf16[256,1024]{1,0:T(8,128)(2,1)} %constant.31.clone.tail_tab) | copy-start | bytes 1572868
  4.9 0.9 %copy-start.3 = (bf16[512,256]{1,0:T(8,128)(2,1)S(1)}, bf16[512,256]{1,0:T(8,128)(2,1)}, u32[]{:S(2)}) copy-start(bf16[512,256]{1,0:T(8,128)(2,1)} %constant.32.clone.grad_rows) | copy-start | bytes 786436
  5.9 0.9 %copy-start.4 = (bf16[512,256]{1,0:T(8,128)(2,1)S(1)}, bf16[512,256]{1,0:T(8,128)(2,1)}, u32[]{:S(2)}) copy-start(bf16[512,256]{1,0:T(8,128)(2,1)} %constant.28.clone.down_cols) | copy-start | bytes 786436
  6.8 0.9 %copy-start.5 = (bf16[1024,128]{1,0:T(8,128)(2,1)S(1)}, bf16[1024,128]{1,0:T(8,128)(2,1)}, u32[]{:S(2)}) copy-start(bf16[1024,128]{1,0:T(8,128)(2,1)} %constant.27.clone.up_rows) | copy-start | bytes 786436
  7.8 0.9 %copy-start.6 = (bf16[256,512]{1,0:T(8,128)(2,1)S(1)}, bf16[256,512]{1,0:T(8,128)(2,1)}, u32[]{:S(2)}) copy-start(bf16[256,512]{1,0:T(8,128)(2,1)} %constant.26.clone.up_cols) | copy-start | bytes 786436
  8.7 0.9 %copy-start.7 = (bf16[512,256]{1,0:T(8,128)(2,1)S(1)}, bf16[512,256]{1,0:T(8,128)(2,1)}, u32[]{:S(2)}) copy-start(bf16[512,256]{1,0:T(8,128)(2,1)} %constant.23.clone.col_side) | copy-start | bytes 786436
  9.7 0.9 %copy-start.9 = (bf16[128,512]{1,0:T(8,128)(2,1)S(1)}, bf16[128,512]{1,0:T(8,128)(2,1)}, u32[]{:S(2)}) copy-start(bf16[128,512]{1,0:T(8,128)(2,1)} %constant.24.clone.lane_fwd) | copy-start | bytes 393220
  10.6 0.9 %copy-start.10 = (bf16[128,512]{1,0:T(8,128)(2,1)S(1)}, bf16[128,512]{1,0:T(8,128)(2,1)}, u32[]{:S(2)}) copy-start(bf16[128,512]{1,0:T(8,128)(2,1)} %constant.22.clone.row_side) | copy-start | bytes 393220
  11.5 0.8 %copy-start.11 = (bf16[128,256]{1,0:T(8,128)(2,1)S(1)}, bf16[128,256]{1,0:T(8,128)(2,1)}, u32[]{:S(2)}) copy-start(bf16[128,256]{1,0:T(8,128)(2,1)} %constant.25.clone.row_fwd) | copy-start | bytes 196612
  12.3 0.8 %copy-start.12 = (bf16[128,128]{1,0:T(8,128)(2,1)S(1)}, bf16[128,128]{1,0:T(8,128)(2,1)}, u32[]{:S(2)}) copy-start(bf16[128,128]{1,0:T(8,128)(2,1)} %constant.29.clone.row_back) | copy-start | bytes 98308

commit v2 on v1

--- a/solution.py
+++ b/solution.py
@@ -86,12 +86,20 @@
 
 def body(
     n, f, edge, count,
-    mask_ref, dual_ref, target_ref, h_ref, w_ref,
-    row_side, col_side, lane_fwd, row_fwd, up_cols, up_rows, down_cols, row_back, lane_back, tail_tab, grad_rows,
-    mask_out, dual_out,
-    shared, ring_s, ring_m, from_h_s, from_h_m, from_v_s, from_v_m, agreed, slope, adj, adj_in,
-    send_sem, recv_sem,
+    *refs,
 ):
+    ins, refs = refs[:16], refs[16:]
+    mask_out, dual_out, common_out = refs[:3]
+    held, refs = refs[3:19], refs[19:]
+    mask_ref, dual_ref, target_ref, k_ref, w_ref = held[:5]
+    row_side, col_side, lane_fwd, row_fwd, up_cols, up_rows, down_cols, row_back, lane_back, tail_tab, grad_rows = held[5:]
+    (
+        h_sc, load_sem, shared, ring_s, ring_m, from_h_s, from_h_m, from_v_s, from_v_m, agreed, slope, adj, adj_in,
+        send_sem, recv_sem,
+    ) = refs
+    loads = [pltpu.make_async_copy(src, dst, load_sem.at[i]) for i, (src, dst) in enumerate(zip(ins, held))]
+    for i in (0, 1, 3, 4, 5, 6, 7, 8, 9, 10, 2, 11, 12, 13, 14, 15):
+        loads[i].start()
     far = n - edge
     g = 2 * f
     me = lax.axis_index("ty")
@@ -173,6 +181,8 @@
         def _(to=to):
             adj_in[to] = jnp.zeros((f, 4 * f), jnp.float32)
 
+    loads[0].wait()
+    loads[1].wait()
     shared[...] = mask_ref[0] + dual_ref[0]
     expected = sum(there.astype(jnp.int32) for _, there in near)
     pl.semaphore_wait(barrier, expected)
@@ -180,6 +190,8 @@
     for entry in plan["s", "h"] + plan["s", "v"] + plan["s", "hm"]:
         start(entry)
 
+    loads[3].wait()
+    loads[4].wait()
     quarters = w_ref.shape[0] // 2
     lane = lax.broadcasted_iota(jnp.int32, (1, 4 * f), 1)
     total = w_ref[0]
@@ -189,11 +201,33 @@
         jnp.where(lane < 2 * f, w_ref[2 * k], w_ref[2 * k + 1]) / jnp.full((1, 4 * f), total, jnp.float32)
         for k in range(quarters)
     ]
-    h_one = h_ref[...]
+    for k in range(quarters):
+        rows_of = []
+        for j in range(4):
+            flat = k_ref.at[2 * k + j // 2]
+            rows_of.append(
+                jnp.concatenate([flat[j % 2 : j % 2 + 1, 4 * f * a : 4 * f * (a + 1)] for a in range(f // 4)], axis=0)
+            )
+        for b in range(4):
+            value = rows_of[b]
+            for j in range(4):
+                if j != b:
+                    value = jnp.where(lane // f == j, pltpu.roll(rows_of[j], (j - b) % 4 * f, 1), value)
+            h_sc[pl.ds(k * f + b, f // 4, stride=4), :] = value
+    h_one = h_sc[...]
     is_real = (lane // f) % 2 == 0
     h_two = jnp.where(is_real, -pltpu.roll(h_one, 3 * f, 1), pltpu.roll(h_one, f, 1))
 
+    waited = set()
+
+    def need(*which):
+        for i in which:
+            if i not in waited:
+                waited.add(i)
+                loads[i].wait()
+
     def fields(mask_low):
+        need(5, 6, 7, 8)
         part = dot(row_side[...], mask_low)
         part = part[: 2 * f] + part[2 * f :]
         grid = dot(jnp.concatenate(split(part), axis=0), col_side[...])
@@ -217,6 +251,7 @@
         return dot(row_fwd[...], stacked(wide)), jnp.concatenate(split(wide), axis=0)
 
     def write_slope(waves):
+        need(9, 10, 2)
         for r in range(0, n, edge):
             real = dot(up_rows[r : r + edge, :], waves)
             imag = dot(up_rows[n + r : n + r + edge, :], waves)
@@ -232,6 +267,7 @@
             slope[r : r + edge, :] = value.astype(BF16)
 
     def adjoint(field):
+        need(11, 12, 13)
         low = dot(up_cols[: 2 * g, :], slope[...])
         low = low[:g] + low[g:]
         low = dot(jnp.concatenate(split(low), axis=0), down_cols[...])
@@ -263,6 +299,7 @@
         return jnp.where(lane < 2 * f, real, imag)
 
     def tails(packed):
+        need(14, 15)
         out = dot(jnp.concatenate(split(packed), axis=1), tail_tab[...])
         return out[:, :n], out[:, n:]
 
@@ -360,10 +397,10 @@
         mean_mask = covered(src_mask, from_h_m, from_v_m, r)
         common = mean_mask - STEP_SIZE * (summed * coverage_part(r) + PENALTY * (mean_mask - before))
         mask = mask_out[0, rows, :]
-        dual = dual_out[0, rows, :] + mask - common
-        dual_out[0, rows, :] = dual
+        dual_out[0, rows, :] = dual_out[0, rows, :] + mask
+        common_out[0, rows, :] = common
         gradient = dot(grad_rows[rows, :], last_stack)
-        mask_out[0, rows, :] = mask - STEP_SIZE * (gradient + PENALTY * (mask - common + dual))
+        mask_out[0, rows, :] = mask - STEP_SIZE * (gradient + PENALTY * (mask - common))
 
     for name in ("s", "m"):
         for part in ("h", "hm", "v", "vc"):
@@ -377,17 +414,23 @@
     n = mask_init.shape[-1]
     edge = INTERSECTION
     f = int(round(kernels.shape[-1] ** 0.5))
-    quarters = kernels.shape[0] // 2
     tables = [jnp.asarray(t) for t in host_tables(n, f)]
-    arranged = kernels.reshape(quarters, 2, 2, f, f).transpose(0, 3, 1, 2, 4).reshape(quarters * f, 4 * f)
     f32 = jnp.float32
     whole = pl.BlockSpec(memory_space=pltpu.VMEM)
-    return pl.pallas_call(
+    far_memory = pl.BlockSpec(memory_space=pltpu.HBM)
+    arrays = (mask_init, dual_init, target, kernels, weights, *tables)
+    tile = jax.ShapeDtypeStruct((1, n, n), f32)
+    ahead, total, common = pl.pallas_call(
         functools.partial(body, n, f, edge, count),
-        out_shape=(jax.ShapeDtypeStruct((1, n, n), f32), jax.ShapeDtypeStruct((1, n, n), f32)),
-        in_specs=[whole] * 4 + [pl.BlockSpec(memory_space=pltpu.SMEM)] + [whole] * len(tables),
-        out_specs=(whole, whole),
+        out_shape=(tile, tile, tile),
+        in_specs=[far_memory] * len(arrays),
+        out_specs=(whole, whole, whole),
         scratch_shapes=[
+            pltpu.SMEM(a.shape, a.dtype) if i == 4 else pltpu.VMEM(a.shape, a.dtype) for i, a in enumerate(arrays)
+        ]
+        + [
+            pltpu.VMEM((kernels.shape[0] // 2 * f, 4 * f), f32),
+            pltpu.SemaphoreType.DMA((len(arrays),)),
             pltpu.VMEM((n, n), f32),
             pltpu.VMEM((2, 2, edge, edge), f32),
             pltpu.VMEM((2, 2, edge, edge), f32),
@@ -403,9 +446,11 @@
             pltpu.SemaphoreType.DMA((40,)),
         ],
         compiler_params=pltpu.CompilerParams(
-            collective_id=0, has_side_effects=True, vmem_limit_bytes=48 * 1024 * 1024
+            collective_id=0, has_side_effects=True, vmem_limit_bytes=67043328
         ),
-    )(mask_init, dual_init, target, arranged, weights, *tables)
+    )(*arrays)
+    dual = total - common
+    return ahead - (STEP_SIZE * PENALTY) * dual, dual
 
 
 def solution(mesh):

time: 36.2 us -> 25.5 us (0.70); the launches traced: 35.6 us -> 25.3 us
  local copies, waits for them, and re-layouts: 14.4 us -> 0 us
  other arithmetic: 0 us -> 3.6 us
  Pallas kernels: 20.5 us -> 21.1 us
    unnamed x30 -> x0, local copies, waits for them, and re-layouts: 12.8 us -> none
    sub x0 -> x1, other arithmetic: none -> 3.6 us  [per_device(): return (ahead - STEP_SIZE * PENALTY * dual, dual)]
    reshape x3 -> x0, local copies, waits for them, and re-layouts: 1.52 us -> none  [per_device(): kernels.reshape(quarters, 2, 2, f, f).transpose(0, 3, 1, 2, 4)]
    pallas_call x1, Pallas kernels: 20.5 us -> 21.1 us  [per_device(): pl.pallas_call(functools.partial(body, n, f, edge, count), out_shape=(til...]
where the time goes in v2:
time: 25.5 us; the launch traced here: 25.3 us
  Pallas kernels  21.1 us (83%)
  other arithmetic  3.6 us (14%)
  between operations  0.64 us (3%)
    pallas_call x1, Pallas kernels, per_device(): pl.pallas_call(functools.partial(body, n, f, edge, count), out_shape=(til...  21.1 us
    sub x1, other arithmetic, per_device(): return (ahead - STEP_SIZE * PENALTY * dual, dual)  3.6 us

profile of v2, /device:TPU:1, one launch (start us, length us, event | category | flops | bytes accessed | tf_op | source)
XLA Modules:
  0.0 25.3 jit_solution(1254870510391313238)
XLA Ops:
  0.6 21.1 %shard_map.167 = (f32[1,512,512]{2,1,0:T(8,128)}, f32[1,512,512]{2,1,0:T(8,128)}, f32[1,512,512]{2,1,0:T(8,128)}) custom-call(f32[1,512,512]{2,1,0:T(8,128)} %refs_0_.1, f32[1,512,512]{2,1,0:T(8,128)} %refs_1_.1, bf16[1,512,512]{2,1,0:T(8,128)(2,1)} %refs_2_.1, f32[8,2,1024]{2,1,0:T(2,128)} %refs_3_.1, f32[8]{0:T(128)} %refs_4_.1, ...), custom_call_target="tpu_custom_call" | custom-call | tf_op jit(solution)/shard_map/pallas_call | solution.py:423
  21.7 3.6 %multiply_subtract_fusion = (f32[1,512,512]{2,1,0:T(8,128)}, f32[1,512,512]{2,1,0:T(8,128)}) fusion(f32[1,512,512]{2,1,0:T(8,128)} %get-tuple-element.5, f32[1,512,512]{2,1,0:T(8,128)} %get-tuple-element.6, f32[1,512,512]{2,1,0:T(8,128)} %get-tuple-element.7), kind=kLoop, calls=%fused_computation | loop fusion | flops 786432 | bytes 5242880 | tf_op jit(solution)/shard_map/sub | solution.py:453

commit v3 on v2

--- a/solution.py
+++ b/solution.py
@@ -89,8 +89,8 @@
     *refs,
 ):
     ins, refs = refs[:16], refs[16:]
-    mask_out, dual_out, common_out = refs[:3]
-    held, refs = refs[3:19], refs[19:]
+    mask_out, dual_out = refs[:2]
+    held, refs = refs[2:18], refs[18:]
     mask_ref, dual_ref, target_ref, k_ref, w_ref = held[:5]
     row_side, col_side, lane_fwd, row_fwd, up_cols, up_rows, down_cols, row_back, lane_back, tail_tab, grad_rows = held[5:]
     (
@@ -397,10 +397,10 @@
         mean_mask = covered(src_mask, from_h_m, from_v_m, r)
         common = mean_mask - STEP_SIZE * (summed * coverage_part(r) + PENALTY * (mean_mask - before))
         mask = mask_out[0, rows, :]
-        dual_out[0, rows, :] = dual_out[0, rows, :] + mask
-        common_out[0, rows, :] = common
+        dual = dual_out[0, rows, :] + mask - common
+        dual_out[0, rows, :] = dual
         gradient = dot(grad_rows[rows, :], last_stack)
-        mask_out[0, rows, :] = mask - STEP_SIZE * (gradient + PENALTY * (mask - common))
+        mask_out[0, rows, :] = mask - STEP_SIZE * (gradient + PENALTY * (mask - common + dual))
 
     for name in ("s", "m"):
         for part in ("h", "hm", "v", "vc"):
@@ -420,11 +420,11 @@
     far_memory = pl.BlockSpec(memory_space=pltpu.HBM)
     arrays = (mask_init, dual_init, target, kernels, weights, *tables)
     tile = jax.ShapeDtypeStruct((1, n, n), f32)
-    ahead, total, common = pl.pallas_call(
+    return pl.pallas_call(
         functools.partial(body, n, f, edge, count),
-        out_shape=(tile, tile, tile),
+        out_shape=(tile, tile),
         in_specs=[far_memory] * len(arrays),
-        out_specs=(whole, whole, whole),
+        out_specs=(whole, whole),
         scratch_shapes=[
             pltpu.SMEM(a.shape, a.dtype) if i == 4 else pltpu.VMEM(a.shape, a.dtype) for i, a in enumerate(arrays)
         ]
@@ -446,11 +446,9 @@
             pltpu.SemaphoreType.DMA((40,)),
         ],
         compiler_params=pltpu.CompilerParams(
-            collective_id=0, has_side_effects=True, vmem_limit_bytes=67043328
+            collective_id=0, has_side_effects=True, vmem_limit_bytes=48 * 1024 * 1024
         ),
-    )(*arrays)
-    dual = total - common
-    return ahead - (STEP_SIZE * PENALTY) * dual, dual
+    )(*[pltpu.with_memory_space_constraint(a, pltpu.HBM) for a in arrays])
 
 
 def solution(mesh):

time: 25.5 us -> 22.2 us (0.87)
  other arithmetic: 3.6 us -> 0 us
  local copies, waits for them, and re-layouts: 0 us -> 1.94 us
  Pallas kernels: 21.1 us -> 19.5 us
    sub x1 -> x0, other arithmetic: 3.6 us -> none  [per_device(): return (ahead - STEP_SIZE * PENALTY * dual, dual)]
    unnamed x0 -> x2, local copies, waits for them, and re-layouts: none -> 1.94 us
    pallas_call x1, Pallas kernels: 21.1 us -> 19.5 us  [per_device(): pl.pallas_call(functools.partial(body, n, f, edge, count), out_shape=(til...]
where the time goes in v3:
time: 22.2 us; the launch traced here: 22 us
  Pallas kernels  19.5 us (88%)
  local copies, waits for them, and re-layouts  1.94 us (9%)
  between operations  0.64 us (3%)
    pallas_call x1, Pallas kernels, per_device(): pl.pallas_call(functools.partial(body, n, f, edge, count), out_shape=(til...  19.5 us
    unnamed x2, local copies, waits for them, and re-layouts  1.94 us

profile of v3, /device:TPU:1, one launch (start us, length us, event | category | flops | bytes accessed | tf_op | source)
XLA Modules:
  0.0 22.0 jit_solution(8322597388646037497)
XLA Ops:
  0.6 19.5 %shard_map.167 = (f32[1,512,512]{2,1,0:T(8,128)S(1)}, f32[1,512,512]{2,1,0:T(8,128)S(1)}) custom-call(f32[1,512,512]{2,1,0:T(8,128)} %refs_0_.1, f32[1,512,512]{2,1,0:T(8,128)} %refs_1_.1, bf16[1,512,512]{2,1,0:T(8,128)(2,1)} %refs_2_.1, f32[8,2,1024]{2,1,0:T(2,128)} %refs_3_.1, f32[8]{0:T(128)} %refs_4_.1, bf16[128,512]{1,0:T(8,128)(2,1)} %constant.22.clone.refs_5_, ...), custom_call_target="tpu_custom_call" | custom-call | tf_op jit(solution)/shard_map/pallas_call | solution.py:423
  20.1 1.0 %copy.20 = f32[1,512,512]{2,1,0:T(8,128)} copy(f32[1,512,512]{2,1,0:T(8,128)S(1)} %get-tuple-element.4) | data formatting | bytes 2097152
  21.1 1.0 %copy.21 = f32[1,512,512]{2,1,0:T(8,128)} copy(f32[1,512,512]{2,1,0:T(8,128)S(1)} %get-tuple-element.5) | data formatting | bytes 2097152
